TPU v7x, 256 devices: a whole 4x4x8 slice. The times are simulated.
256 devices in a mesh: lat: 16 (over y, x), kpt: 16 (over z, core).
Axes of the slice: x: 4, y: 4, z: 8, core: 2. Of those that a mesh axis runs over, the one named last changes fastest.
Arguments:
- coarse: bfloat16 [2, 16, 256, 12288], P(None, 'lat', 'kpt'), may hold values from -0.1875 to 0.1875
- rp_vectors: int32 [16, 3], P('lat'), may hold values from -4 to 4
- rp_weights: int32 [16], P('lat'), may hold values from 1 to 3
- re_vectors: int32 [256, 3], replicated, may hold values from -4 to 4
- re_weights: int32 [256], replicated, may hold values from 1 to 3
- q_points: float32 [2, 3], replicated, may hold values from 0 to 1
- k_points: float32 [1024, 3], P('kpt'), may hold values from 0 to 1
- modes_rot: bfloat16 [2, 2, 48, 48], replicated, may hold values from -0.625 to 0.625
- u_k: bfloat16 [2, 1024, 16, 16], P(None, 'kpt'), may hold values from -1 to 1
- u_kq: bfloat16 [2, 2, 1024, 16, 16], P(None, None, 'kpt'), may hold values from -1 to 1
- mask_k: int32 [1024, 16], P('kpt'), may hold values 0 or 1
- mask_kq: int32 [2, 1024, 16], P(None, 'kpt'), may hold values 0 or 1
Outputs:
- coupling: bfloat16 [2, 1024, 2, 12288], P(None, 'kpt', None, 'lat')
All inputs are finite; a program needn't handle non-finite values. No bound on the sum of `mask_k` or of `mask_kq` on one device may be relied on, other than what follows from the above.
Results may differ from a plain program's by a relative error of at most 0.017.
Values may be sent and summed in bfloat16 or wider, within the bound.
No kernel may reach another device: no remote copies, remote signals or barrier semaphores. Data moves between devices by JAX's collectives and lax.ppermute only.
A program may use at most 64 MiB of HBM per device.

v0:
```python
import jax
import jax.numpy as jnp
from jax import lax
from jax.sharding import PartitionSpec as P

two_pi = 6.283185307179586


def phases(points, vectors, weights):
    cells = vectors.astype(jnp.float32)
    argument = two_pi * (
        points[:, 0:1] * cells[None, :, 0]
        + points[:, 1:2] * cells[None, :, 1]
        + points[:, 2:3] * cells[None, :, 2]
    )
    inverse = 1.0 / weights.astype(jnp.float32)
    return (
        (jnp.cos(argument) * inverse).astype(jnp.bfloat16),
        (jnp.sin(argument) * inverse).astype(jnp.bfloat16),
    )


def rotate_modes(values, modes_rot):
    shape = values.shape
    mode_count = modes_rot.shape[2]
    split = values.reshape(shape[0], shape[1], shape[2], mode_count, shape[3] // mode_count)
    br = jnp.einsum(
        "qmn,qrmx->qrnx", modes_rot[0], split[0], preferred_element_type=jnp.float32
    ) - jnp.einsum("qmn,qrmx->qrnx", modes_rot[1], split[1], preferred_element_type=jnp.float32)
    bi = jnp.einsum(
        "qmn,qrmx->qrnx", modes_rot[0], split[1], preferred_element_type=jnp.float32
    ) + jnp.einsum("qmn,qrmx->qrnx", modes_rot[1], split[0], preferred_element_type=jnp.float32)
    return jnp.stack([br, bi]).reshape(shape).astype(jnp.bfloat16)


def phonon_sum(block, vectors, weights, q_points):
    phase_real, phase_imag = phases(q_points, vectors, weights)
    rows = block.shape[1]
    cells = block.shape[2]
    lanes = block.shape[3]
    flat_real = block[0].reshape(rows, cells * lanes)
    flat_imag = block[1].reshape(rows, cells * lanes)
    part_real = jnp.dot(phase_real, flat_real, preferred_element_type=jnp.float32) - jnp.dot(
        phase_imag, flat_imag, preferred_element_type=jnp.float32
    )
    part_imag = jnp.dot(phase_real, flat_imag, preferred_element_type=jnp.float32) + jnp.dot(
        phase_imag, flat_real, preferred_element_type=jnp.float32
    )
    return jnp.stack([part_real, part_imag]).reshape(2, q_points.shape[0], cells, lanes)


def per_device(
    coarse,
    rp_vectors,
    rp_weights,
    re_vectors,
    re_weights,
    q_points,
    k_points,
    modes_rot,
    u_k,
    u_kq,
    mask_k,
    mask_kq,
):
    q_count = q_points.shape[0]
    k_count = k_points.shape[0]
    band_count = u_k.shape[2]
    partial_value = phonon_sum(coarse, rp_vectors, rp_weights, q_points)
    summed = lax.psum_scatter(partial_value, "lat", scatter_dimension=2, tiled=True).astype(
        jnp.bfloat16
    )
    rotated = rotate_modes(summed, modes_rot)
    shared = lax.all_to_all(rotated, "lat", split_axis=3, concat_axis=2, tiled=True)
    lane_local = shared.shape[3]
    portion = lax.all_gather(shared, "kpt", axis=2, tiled=True)
    kreal, kimag = phases(k_points, re_vectors, re_weights)
    er = jnp.einsum(
        "kr,qrx->kqx", kreal, portion[0], preferred_element_type=jnp.float32
    ) - jnp.einsum("kr,qrx->kqx", kimag, portion[1], preferred_element_type=jnp.float32)
    ei = jnp.einsum(
        "kr,qrx->kqx", kreal, portion[1], preferred_element_type=jnp.float32
    ) + jnp.einsum("kr,qrx->kqx", kimag, portion[0], preferred_element_type=jnp.float32)
    totals = jnp.stack([er, ei])
    mode_local = lane_local // (band_count * band_count)
    field = totals.astype(jnp.bfloat16).reshape(
        2, k_count, q_count, mode_local, band_count, band_count
    )
    tr = jnp.einsum(
        "kqmab,kbn->kqman", field[0], u_k[0], preferred_element_type=jnp.float32
    ) - jnp.einsum("kqmab,kbn->kqman", field[1], u_k[1], preferred_element_type=jnp.float32)
    ti = jnp.einsum(
        "kqmab,kbn->kqman", field[0], u_k[1], preferred_element_type=jnp.float32
    ) + jnp.einsum("kqmab,kbn->kqman", field[1], u_k[0], preferred_element_type=jnp.float32)
    tr = tr.astype(jnp.bfloat16)
    ti = ti.astype(jnp.bfloat16)
    outr = jnp.einsum(
        "qkac,kqman->kqmcn", u_kq[0], tr, preferred_element_type=jnp.float32
    ) + jnp.einsum("qkac,kqman->kqmcn", u_kq[1], ti, preferred_element_type=jnp.float32)
    outi = jnp.einsum(
        "qkac,kqman->kqmcn", u_kq[0], ti, preferred_element_type=jnp.float32
    ) - jnp.einsum("qkac,kqman->kqmcn", u_kq[1], tr, preferred_element_type=jnp.float32)
    window = (
        jnp.transpose(mask_kq.astype(jnp.float32), (1, 0, 2))[:, :, None, :, None]
        * mask_k.astype(jnp.float32)[:, None, None, None, :]
    )
    result = jnp.stack([outr * window, outi * window])
    return result.reshape(2, k_count, q_count, lane_local).astype(jnp.bfloat16)


def solution(mesh):
    placed = (
        P(None, "lat", "kpt", None),
        P("lat", None),
        P("lat"),
        P(),
        P(),
        P(),
        P("kpt", None),
        P(),
        P(None, "kpt", None, None),
        P(None, None, "kpt", None, None),
        P("kpt", None),
        P(None, "kpt", None),
    )
    return jax.shard_map(
        per_device,
        mesh=mesh,
        in_specs=placed,
        out_specs=P(None, "kpt", None, "lat"),
        check_vma=False,
    )
```

profile of v0, /device:TPU:1, one launch (start us, length us, event | category | flops | bytes accessed | tf_op | source)
XLA Modules:
  0.0 256.3 jit_solution(5092199044945277099)
XLA Ops:
  7.2 0.7 convert_element_type.53
  7.8 0.6 fusion.56
  8.5 1.2 convert_bitcast_fusion.1
  10.1 0.3 copy-done.10
  10.4 2.1 convert_reduce_fusion.1
  12.4 1.5 multiply_subtract_fusion
  13.9 1.4 pad_maximum_fusion
  15.4 86.5 %all-reduce.2 = bf16[2,2,16,12288]{3,1,2,0:T(2,128)(2,1)} all-reduce(f32[2,2,16,12288]{3,1,2,0:T(2,128)S(1)} %pad_maximum_fusion), channel_id=2, replica_groups=mesh['lat'=16,'kpt'=16] {'lat'}, use_global_device_ids=true, to_apply=%region_0.0.clone | all-reduce | flops 786432 | bytes 4718592
  101.9 0.6 dynamic-slice
  102.5 1.6 dynamic-slice_convert_fusion
  104.6 0.2 fusion.4
  104.8 0.2 fusion.5
  105.1 10.0 %copy.99 = bf16[2,2,1,12288]{1,0,2,3:T(2,128)(2,1)} copy(bf16[2,2,1,12288]{3,1,2,0:T(2,128)(2,1)S(1)} %pad_maximum_fusion.2) | data formatting | bytes 196608 | tf_op jit(solution)/shard_map/stack | solution.py:33
  115.1 13.7 %reshape.158 = bf16[16,2,1536]{2,1,0:T(2,128)(2,1)S(1)} reshape(bf16[12288,1,2,2]{3,2,1,0:T(2,128)(2,1)} %bitcast.147) | data formatting | bytes 196608
  128.8 9.2 %all_to_all.12 = bf16[16,2,1536]{2,1,0:T(2,128)(2,1)S(1)} all-to-all(bf16[16,2,1536]{2,1,0:T(2,128)(2,1)S(1)} %reshape.158), channel_id=1, replica_groups=mesh['lat'=16,'kpt'=16] {'lat'}, dimensions={0} | all-to-all | bytes 196608 | tf_op jit(solution)/shard_map/all_to_all | solution.py:74
  138.0 14.7 %reshape.159 = bf16[12288,1,2,2]{3,2,1,0:T(2,128)(2,1)} reshape(bf16[16,2,1536]{2,1,0:T(2,128)(2,1)S(1)} %all_to_all.12) | data formatting | bytes 196608
  152.8 9.9 %copy.128 = bf16[2,2,16,768]{3,2,1,0:T(8,128)(2,1)} copy(bf16[2,2,16,768]{1,0,3,2:T(2,128)(2,1)} %bitcast.148) | data formatting | bytes 196608 | tf_op jit(solution)/shard_map/all_to_all | solution.py:74
  162.8 0.3 copy.133
  163.0 1.0 copy.134
  164.0 1.5 copy.136
  165.5 1.5 copy.135
  167.1 0.7 broadcast_multiply_fusion
  167.8 45.9 %all-gather.2.cloned.1.call-done = bf16[2,2,256,768]{3,2,1,0:T(8,128)(2,1)} async-done(((bf16[2,2,16,768]{3,2,1,0:T(8,128)(2,1)}), bf16[2,2,256,768]{3,2,1,0:T(8,128)(2,1)}) %all-gather.2.cloned.1.call-update) | async-done | bytes 1572880 | tf_op jit(solution)/shard_map/all_gather | solution.py:76
  213.8 1.7 fusion.9
  215.5 1.6 fusion.1
  217.1 0.9 copy.104
  218.1 0.5 fusion.8
  218.6 0.5 fusion
  219.1 0.2 copy.101
  219.3 1.3 copy.103
  220.6 2.2 copy.106
  222.8 1.5 fusion.21
  224.3 0.5 fusion.19
  224.8 0.5 add_convert_fusion
  225.4 0.4 copy-done.4
  225.8 0.6 subtract_convert_fusion
  226.3 0.5 copy-done.2
  226.8 2.4 fusion.10
  229.2 0.6 fusion.16
  229.8 2.3 fusion.14
  232.1 2.3 fusion.12
  234.4 3.4 %copy.118 = f32[64,2,3,16,16]{0,3,4,2,1:T(8,128)} copy(f32[64,2,3,16,16]{4,3,2,1,0:T(8,128)} %fusion.10) | data formatting | bytes 786432 | tf_op jit(solution)/shard_map/qkac,kqman->kqmcn/dot_general | solution.py:102
  237.9 2.3 copy.113
  240.1 3.6 %copy.117 = f32[64,2,3,16,16]{0,3,4,2,1:T(8,128)} copy(f32[64,2,3,16,16]{4,3,2,1,0:T(8,128)} %fusion.14) | data formatting | bytes 786432 | tf_op jit(solution)/shard_map/qkac,kqman->kqmcn/dot_general | solution.py:100
  243.8 2.3 copy.114
  246.1 2.1 fusion.7
  248.1 0.2 pad_maximum_fusion.1
  248.3 1.1 copy.119
  (47 shorter events, 1.0 us)
Async XLA Ops:
  6.5 207.2 %all-gather.2.cloned.1.call-start = ((), (), s32[]{:S(2)}) async-start(), calls=%async_computation.1 | async-start | bytes 1671168 | tf_op jit(solution)/shard_map/all_gather | solution.py:76
  9.7 0.7 copy-start.10
  15.3 86.6 %copy-start.15 = (u32[256]{0:T(256)S(1)}, u32[256]{0:T(256)}, u32[]{:S(2)}) copy-start(u32[256]{0:T(256)} %constant.12) | copy-start | bytes 3076
  15.4 88.8 %copy-start.7 = (bf16[2,2,48,48]{3,2,1,0:T(8,128)(2,1)S(1)}, bf16[2,2,48,48]{3,2,1,0:T(8,128)(2,1)}, u32[]{:S(2)}) copy-start(bf16[2,2,48,48]{3,2,1,0:T(8,128)(2,1)} %param.19) | copy-start | bytes 55300
  152.7 9.9 %copy-start.12 = (s32[256,3]{0,1:T(4,128)S(1)}, s32[256,3]{0,1:T(4,128)}, u32[]{:S(2)}) copy-start(s32[256,3]{0,1:T(4,128)} %param.15) | copy-start | bytes 9220
  152.7 10.0 %copy-start.11 = (s32[64,16]{0,1:T(8,128)S(1)}, s32[64,16]{0,1:T(8,128)}, u32[]{:S(2)}) copy-start(s32[64,16]{0,1:T(8,128)} %param.22) | copy-start | bytes 12292
  152.8 10.0 %copy-start.8 = (bf16[2,64,16,16]{1,3,2,0:T(8,128)(2,1)S(1)}, bf16[2,64,16,16]{1,3,2,0:T(8,128)(2,1)}, u32[]{:S(2)}) copy-start(bf16[2,64,16,16]{1,3,2,0:T(8,128)(2,1)} %param.20) | copy-start | bytes 196612
  152.8 11.2 %copy-start.6 = (bf16[2,2,64,16,16]{2,4,3,1,0:T(8,128)(2,1)S(1)}, bf16[2,2,64,16,16]{2,4,3,1,0:T(8,128)(2,1)}, u32[]{:S(2)}) copy-start(bf16[2,2,64,16,16]{2,4,3,1,0:T(8,128)(2,1)} %param.21) | copy-start | bytes 393220
  162.6 4.4 %copy-start.14 = (s32[256]{0:T(256)S(1)}, s32[256]{0:T(256)}, u32[]{:S(2)}) copy-start(s32[256]{0:T(256)} %param.16) | copy-start | bytes 3076
  162.7 4.4 %copy-start.13 = (f32[64,3]{0,1:T(4,128)S(1)}, f32[64,3]{0,1:T(4,128)}, u32[]{:S(2)}) copy-start(f32[64,3]{0,1:T(4,128)} %param.18) | copy-start | bytes 2308
  162.7 4.5 %copy-start.9 = (s32[2,64,16]{1,2,0:T(8,128)S(1)}, s32[2,64,16]{1,2,0:T(8,128)}, u32[]{:S(2)}) copy-start(s32[2,64,16]{1,2,0:T(8,128)} %param.23) | copy-start | bytes 24580
  213.7 4.3 %copy-start.1 = (bf16[2,2,256,768]{3,2,1,0:T(8,128)(2,1)S(1)}, bf16[2,2,256,768]{3,2,1,0:T(8,128)(2,1)}, u32[]{:S(2)}) copy-start(bf16[2,2,256,768]{3,2,1,0:T(8,128)(2,1)} %all-gather.2.cloned.1.call-done) | copy-start | bytes 4718596
  224.8 1.0 copy-start.4
  225.8 1.0 copy-start.2
  226.8 2.4 copy-start.3
  240.1 3.6 %copy-start = (f32[64,2,3,16,16]{4,3,2,1,0:T(8,128)S(1)}, f32[64,2,3,16,16]{4,3,2,1,0:T(8,128)}, u32[]{:S(2)}) copy-start(f32[64,2,3,16,16]{4,3,2,1,0:T(8,128)} %fusion.12) | copy-start | bytes 1179652
  243.8 2.3 copy-start.5
Sparse Core Ops, SparseCore 0:
  162.8 50.9 all-gather.1
where the time goes:
time: 257 us; the launch traced here: 256 us
  blocking collectives  95.8 us (37%)
  local copies, waits for them, and re-layouts  74.4 us (29%)
  waiting for transfers between devices  45.9 us (18%)
  matrix products  15.8 us (6%)
  between operations  14.4 us (6%)
  other arithmetic  9.95 us (4%)
    unnamed x1, blocking collectives  86.5 us
    all_gather x1, waiting for transfers between devices, per_device(): portion = lax.all_gather(shared, 'kpt', axis=2, tiled=True)  45.9 us
    unnamed x41, local copies, waits for them, and re-layouts  34.8 us
    another operation x3, local copies, waits for them, and re-layouts, rotate_modes(): return jnp.stack([br, bi]).reshape(shape).astype(jnp.bfloat16)  10 us
    all_to_all x1, local copies, waits for them, and re-layouts, per_device(): lax.all_to_all(rotated, 'lat', split_axis=3, concat_axis=2, tiled=True)  9.89 us
    all_to_all x1, blocking collectives, per_device(): lax.all_to_all(rotated, 'lat', split_axis=3, concat_axis=2, tiled=True)  9.25 us
  transfers between devices with their start and end apart: 1, of which 1 were waited for; matrix products, arithmetic and copies ran while one was open for 2% of the time, Pallas kernels for 0%

commit v1 on v0

--- a/solution.py
+++ b/solution.py
@@ -2,6 +2,7 @@
 import jax.numpy as jnp
 from jax import lax
 from jax.sharding import PartitionSpec as P
+from jax.lax import all_to_all, psum
 
 two_pi = 6.283185307179586
 
@@ -71,7 +72,15 @@
         jnp.bfloat16
     )
     rotated = rotate_modes(summed, modes_rot)
-    shared = lax.all_to_all(rotated, "lat", split_axis=3, concat_axis=2, tiled=True)
+    shared = jnp.concatenate(
+        all_to_all(
+            jnp.stack(jnp.split(rotated, psum(1, "lat"), axis=3)),
+            "lat",
+            concat_axis=0,
+            split_axis=0,
+        ),
+        axis=2,
+    )
     lane_local = shared.shape[3]
     portion = lax.all_gather(shared, "kpt", axis=2, tiled=True)
     kreal, kimag = phases(k_points, re_vectors, re_weights)

time: 257 us -> 209 us (0.81)
  local copies, waits for them, and re-layouts: 74.4 us -> 26.8 us
    unnamed x41 -> x39, local copies, waits for them, and re-layouts: 34.8 us -> 6.42 us
    another operation x3 -> x2, local copies, waits for them, and re-layouts: 10 us -> 0.04 us  [rotate_modes(): return jnp.stack([br, bi]).reshape(shape).astype(jnp.bfloat16)]
    all_to_all x1, local copies, waits for them, and re-layouts: 9.89 us -> 0.65 us  [per_device(): all_to_all(jnp.stack(jnp.split(rotated, psum(1, 'lat'), axis=3)), 'lat',...]
where the time goes in v1:
time: 209 us
  blocking collectives  95.8 us (46%)
  waiting for transfers between devices  45.9 us (22%)
  local copies, waits for them, and re-layouts  26.8 us (13%)
  matrix products  15.8 us (8%)
  between operations  14.5 us (7%)
  other arithmetic  10.1 us (5%)
    unnamed x1, blocking collectives  86.5 us
    all_gather x1, waiting for transfers between devices, per_device(): portion = lax.all_gather(shared, 'kpt', axis=2, tiled=True)  45.9 us
    all_to_all x1, blocking collectives, per_device(): all_to_all(jnp.stack(jnp.split(rotated, psum(1, 'lat'), axis=3)), 'lat',...  9.25 us
    unnamed x39, local copies, waits for them, and re-layouts  6.42 us
  transfers between devices with their start and end apart: 1, of which 1 were waited for; matrix products, arithmetic and copies ran while one was open for 2% of the time, Pallas kernels for 0%

profile of v1, /device:TPU:1, one launch (start us, length us, event | category | flops | bytes accessed | tf_op | source)
XLA Modules:
  0.0 208.8 jit_solution(9630728916496115983)
XLA Ops:
  7.2 0.7 convert_element_type.53
  7.8 0.6 fusion.57
  8.5 1.2 convert_bitcast_fusion.1
  9.7 0.2 copy.721
  10.1 0.3 copy-done.10
  10.4 2.1 convert_reduce_fusion.1
  12.4 1.5 multiply_subtract_fusion
  13.9 1.4 pad_maximum_fusion
  15.4 86.5 %all-reduce.2 = bf16[2,2,16,12288]{3,1,2,0:T(2,128)(2,1)} all-reduce(f32[2,2,16,12288]{3,1,2,0:T(2,128)S(1)} %pad_maximum_fusion), channel_id=3, replica_groups=mesh['lat'=16,'kpt'=16] {'lat'}, use_global_device_ids=true, to_apply=%region_0.0.clone | all-reduce | flops 786432 | bytes 4718592
  101.9 0.6 dynamic-slice
  102.5 1.6 dynamic-slice_convert_fusion
  104.2 0.2 fusion.25
  104.4 0.2 fusion.27
  104.6 0.2 fusion.4
  104.8 0.2 fusion.5
  105.3 9.2 %all_to_all.5 = bf16[16,2,2,1,768]{4,2,3,1,0:T(2,128)(2,1)S(1)} all-to-all(bf16[16,2,2,1,768]{4,2,3,1,0:T(2,128)(2,1)S(1)} %bitcast.259), channel_id=1, replica_groups=mesh['lat'=16,'kpt'=16] {'lat'}, dimensions={0} | all-to-all | bytes 196608 | tf_op jit(solution)/shard_map/all_to_all | solution.py:76
  114.6 0.7 copy.742
  115.3 0.3 copy.717
  115.6 1.0 copy.718
  116.6 1.5 copy.720
  118.1 1.5 copy.719
  119.7 0.7 broadcast_multiply_fusion
  120.4 45.9 %all-gather.3.cloned.1.call-done = bf16[2,2,256,1,768]{4,2,1,3,0:T(8,128)(2,1)} async-done(((bf16[2,2,16,1,768]{4,2,1,3,0:T(8,128)(2,1)}), bf16[2,2,256,1,768]{4,2,1,3,0:T(8,128)(2,1)}) %all-gather.3.cloned.1.call-update) | async-done | bytes 1572880 | tf_op jit(solution)/shard_map/all_gather | solution.py:85
  166.3 1.7 fusion.9
  168.1 1.6 fusion.1
  169.7 0.9 copy.689
  170.6 0.5 fusion.8
  171.1 0.5 fusion
  171.6 0.2 copy.686
  171.9 1.3 copy.688
  173.2 2.2 %copy.691 = bf16[64,2,3,16,16]{4,3,2,1,0:T(8,128)(2,1)S(1)} copy(bf16[64,2,3,16,16]{0,4,3,2,1:T(8,128)(2,1)} %bitcast.252) | data formatting | bytes 393216 | tf_op jit(solution)/shard_map/squeeze | solution.py:100
  175.3 1.5 fusion.21
  176.8 0.5 fusion.19
  177.4 0.5 add_convert_fusion
  177.9 0.4 copy-done.4
  178.3 0.5 subtract_convert_fusion
  178.9 0.5 copy-done.2
  179.4 2.3 %fusion.10 = f32[64,2,3,16,16]{4,3,2,1,0:T(8,128)} fusion(bf16[64,2,3,16,16]{4,3,2,1,0:T(8,128)(2,1)S(1)} %subtract_convert_fusion, bf16[1,2,64,16,16]{4,3,1,2,0:T(8,128)(2,1)S(1)} %copy-done.2), kind=kOutput, calls=%fused_computation.26 | convolution fusion | flops 3145728 | bytes 655360 | tf_op jit(solution)/shard_map/qkac,kqman->kqmcn/dot_general | solution.py:111
  181.7 0.6 fusion.16
  182.4 2.3 %fusion.14 = f32[64,2,3,16,16]{4,3,2,1,0:T(8,128)} fusion(bf16[64,2,3,16,16]{4,3,2,1,0:T(8,128)(2,1)S(1)} %add_convert_fusion, bf16[1,2,64,16,16]{4,3,1,2,0:T(8,128)(2,1)S(1)} %copy-done.3), kind=kOutput, calls=%fused_computation.30 | convolution fusion | flops 3145728 | bytes 655360 | tf_op jit(solution)/shard_map/qkac,kqman->kqmcn/dot_general | solution.py:109
  184.7 2.3 %fusion.12 = f32[64,2,3,16,16]{4,3,2,1,0:T(8,128)} fusion(bf16[64,2,3,16,16]{4,3,2,1,0:T(8,128)(2,1)S(1)} %add_convert_fusion, bf16[1,2,64,16,16]{4,3,1,2,0:T(8,128)(2,1)S(1)} %copy-done.2), kind=kOutput, calls=%fused_computation.28 | convolution fusion | flops 3145728 | bytes 655360 | tf_op jit(solution)/shard_map/qkac,kqman->kqmcn/dot_general | solution.py:108
  187.0 3.4 %copy.703 = f32[64,2,3,16,16]{0,3,4,2,1:T(8,128)} copy(f32[64,2,3,16,16]{4,3,2,1,0:T(8,128)} %fusion.10) | data formatting | bytes 786432 | tf_op jit(solution)/shard_map/qkac,kqman->kqmcn/dot_general | solution.py:111
  190.4 2.3 %copy.698 = f32[64,2,3,16,16]{0,3,4,2,1:T(8,128)} copy(f32[64,2,3,16,16]{4,3,2,1,0:T(8,128)S(1)} %fusion.16) | data formatting | bytes 786432 | tf_op jit(solution)/shard_map/qkac,kqman->kqmcn/dot_general | solution.py:106
  192.7 3.6 %copy.702 = f32[64,2,3,16,16]{0,3,4,2,1:T(8,128)} copy(f32[64,2,3,16,16]{4,3,2,1,0:T(8,128)} %fusion.14) | data formatting | bytes 786432 | tf_op jit(solution)/shard_map/qkac,kqman->kqmcn/dot_general | solution.py:109
  196.3 2.3 %copy.699 = f32[64,2,3,16,16]{0,3,4,2,1:T(8,128)} copy(f32[64,2,3,16,16]{4,3,2,1,0:T(8,128)S(1)} %copy-done) | data formatting | bytes 786432 | tf_op jit(solution)/shard_map/qkac,kqman->kqmcn/dot_general | solution.py:108
  198.6 2.1 fusion.7
  200.7 0.2 pad_maximum_fusion.1
  200.9 1.1 copy.704
  (59 shorter events, 0.7 us)
Async XLA Ops:
  6.5 159.8 %all-gather.3.cloned.1.call-start = ((), (), s32[]{:S(2)}) async-start(), calls=%async_computation.1 | async-start | bytes 1671168 | tf_op jit(solution)/shard_map/all_gather | solution.py:85
  9.7 0.7 copy-start.10
  15.3 86.6 %copy-start.15 = (u32[256]{0:T(256)S(1)}, u32[256]{0:T(256)}, u32[]{:S(2)}) copy-start(u32[256]{0:T(256)} %constant.12) | copy-start | bytes 3076
  15.4 88.8 %copy-start.7 = (bf16[2,2,48,48]{3,2,1,0:T(8,128)(2,1)S(1)}, bf16[2,2,48,48]{3,2,1,0:T(8,128)(2,1)}, u32[]{:S(2)}) copy-start(bf16[2,2,48,48]{3,2,1,0:T(8,128)(2,1)} %param.19) | copy-start | bytes 55300
  104.2 11.0 %copy-start.12 = (s32[256,3]{0,1:T(4,128)S(1)}, s32[256,3]{0,1:T(4,128)}, u32[]{:S(2)}) copy-start(s32[256,3]{0,1:T(4,128)} %param.15) | copy-start | bytes 9220
  104.2 11.1 %copy-start.11 = (s32[64,16]{0,1:T(8,128)S(1)}, s32[64,16]{0,1:T(8,128)}, u32[]{:S(2)}) copy-start(s32[64,16]{0,1:T(8,128)} %param.22) | copy-start | bytes 12292
  104.2 11.1 %copy-start.8 = (bf16[2,64,16,16]{1,3,2,0:T(8,128)(2,1)S(1)}, bf16[2,64,16,16]{1,3,2,0:T(8,128)(2,1)}, u32[]{:S(2)}) copy-start(bf16[2,64,16,16]{1,3,2,0:T(8,128)(2,1)} %param.20) | copy-start | bytes 196612
  105.0 11.5 %copy-start.6 = (bf16[2,2,64,16,16]{2,4,3,1,0:T(8,128)(2,1)S(1)}, bf16[2,2,64,16,16]{2,4,3,1,0:T(8,128)(2,1)}, u32[]{:S(2)}) copy-start(bf16[2,2,64,16,16]{2,4,3,1,0:T(8,128)(2,1)} %param.21) | copy-start | bytes 393220
  114.6 5.1 %copy-start.14 = (s32[256]{0:T(256)S(1)}, s32[256]{0:T(256)}, u32[]{:S(2)}) copy-start(s32[256]{0:T(256)} %param.16) | copy-start | bytes 3076
  114.6 5.1 %copy-start.13 = (f32[64,3]{0,1:T(4,128)S(1)}, f32[64,3]{0,1:T(4,128)}, u32[]{:S(2)}) copy-start(f32[64,3]{0,1:T(4,128)} %param.18) | copy-start | bytes 2308
  114.6 5.1 %copy-start.9 = (s32[2,64,16]{1,2,0:T(8,128)S(1)}, s32[2,64,16]{1,2,0:T(8,128)}, u32[]{:S(2)}) copy-start(s32[2,64,16]{1,2,0:T(8,128)} %param.23) | copy-start | bytes 24580
  166.3 4.3 %copy-start.1 = (bf16[2,2,256,1,768]{4,2,1,3,0:T(8,128)(2,1)S(1)}, bf16[2,2,256,1,768]{4,2,1,3,0:T(8,128)(2,1)}, u32[]{:S(2)}) copy-start(bf16[2,2,256,1,768]{4,2,1,3,0:T(8,128)(2,1)} %all-gather.3.cloned.1.call-done) | copy-start | bytes 4718596
  177.4 1.0 copy-start.4
  178.3 1.0 copy-start.2
  179.4 2.4 %copy-start.3 = (bf16[1,2,64,16,16]{4,3,1,2,0:T(8,128)(2,1)S(1)}, bf16[1,2,64,16,16]{4,3,1,2,0:T(8,128)(2,1)}, u32[]{:S(2)}) copy-start(bf16[1,2,64,16,16]{4,3,1,2,0:T(8,128)(2,1)} %copy.719) | copy-start | bytes 196612
  192.7 3.6 %copy-start = (f32[64,2,3,16,16]{4,3,2,1,0:T(8,128)S(1)}, f32[64,2,3,16,16]{4,3,2,1,0:T(8,128)}, u32[]{:S(2)}) copy-start(f32[64,2,3,16,16]{4,3,2,1,0:T(8,128)} %fusion.12) | copy-start | bytes 1179652
  196.3 2.3 %copy-start.5 = (f32[64,2,16,16]{0,3,2,1:T(8,128)S(1)}, f32[64,2,16,16]{0,3,2,1:T(8,128)}, u32[]{:S(2)}) copy-start(f32[64,2,16,16]{0,3,2,1:T(8,128)} %broadcast_multiply_fusion) | copy-start | bytes 393220
Sparse Core Ops, SparseCore 0:
  115.4 50.9 all-gather.2
